TPU v7x, 256 devices: a whole 4x4x8 slice. The times are simulated.
256 devices in a mesh: dom: 16 (over y, z_lo, core), dir: 16 (over x, z_hi).
Axes of the slice: x: 4, y: 4, z: 8 (z_hi: 4, z_lo: 2; z = z_hi * 2 + z_lo), core: 2. Of those that a mesh axis runs over, the one named last changes fastest.
Arguments:
- coefficients: bfloat16 [2, 70, 32768], P(None, None, ('dom', 'dir')), may hold values from -6 to 6
- positions: float32 [3, 32768], P(None, ('dom', 'dir')), may hold values from -50 to 50
- polar: float32 [10240], P('dir'), may hold values from 0 to 1.4
- azimuth: float32 [10240], P('dir'), may hold values from -3.140625 to 3.140625
- weights: float32 [10240], P('dir'), may hold values from -4 to 4
- farmap: float32 [2, 2, 70, 10240], P(None, None, None, 'dir'), may hold values from -0.00390625 to 0.00390625
Outputs:
- coef_grad: float32 [2, 70, 32768], P(None, None, ('dom', 'dir'))
- place_grad: float32 [3, 32768], P(None, ('dom', 'dir'))
All inputs are finite; a program needn't handle non-finite values.
Results may differ from a plain program's by a relative error of at most 0.0052.
Values may be sent and summed in bfloat16 or wider, within the bound.
A program may use at most 64 MiB of HBM per device.

v0:
```python
import jax
import jax.numpy as jnp
from jax import lax
from jax.sharding import PartitionSpec as P

C = 70


def unit_vectors(polar, azimuth):
    sine_polar = jnp.sin(polar)
    return jnp.stack([sine_polar * jnp.cos(azimuth), sine_polar * jnp.sin(azimuth), jnp.cos(polar)])


def phase_tile(places, vectors):
    angles = (
        places[0][:, None] * vectors[0][None, :]
        + places[1][:, None] * vectors[1][None, :]
        + places[2][:, None] * vectors[2][None, :]
    )
    return (jnp.cos(angles).astype(jnp.bfloat16), jnp.sin(angles).astype(jnp.bfloat16))


def field_terms(coef_block, cos_tile, sin_tile):
    order_count = coef_block.shape[0] // 2
    real_rows = coef_block[:order_count]
    imag_rows = coef_block[order_count:]
    top_rows = jnp.concatenate([real_rows, imag_rows], axis=1)
    low_rows = jnp.concatenate([imag_rows, -real_rows], axis=1)
    left_side = jnp.concatenate([top_rows, low_rows], axis=0)
    right_side = jnp.concatenate([cos_tile, sin_tile], axis=0)
    return jnp.dot(left_side, right_side, preferred_element_type=jnp.float32)


def adjoint_terms(stacked, cos_tile, sin_tile):
    order_count = stacked.shape[0] // 2
    real_rows = stacked[:order_count]
    imag_rows = stacked[order_count:]
    top_rows = jnp.concatenate([real_rows, imag_rows], axis=1)
    low_rows = jnp.concatenate([imag_rows, -real_rows], axis=1)
    left_side = jnp.concatenate([top_rows, low_rows], axis=0)
    right_side = jnp.concatenate([cos_tile, sin_tile], axis=1)
    return lax.dot_general(
        left_side, right_side, (((1,), (1,)), ((), ())), preferred_element_type=jnp.float32
    )


def amplitude_parts(fields, farmap):
    order_count = fields.shape[0] // 2
    field_real = fields[:order_count][None]
    field_imag = fields[order_count:][None]
    map_real = farmap[:, 0]
    map_imag = farmap[:, 1]
    amp_real = jnp.sum(map_real * field_real - map_imag * field_imag, axis=1)
    amp_imag = jnp.sum(map_real * field_imag + map_imag * field_real, axis=1)
    return (amp_real, amp_imag)


def cotangent_from(amp_real, amp_imag, farmap, weights):
    map_real = farmap[:, 0]
    map_imag = farmap[:, 1]
    cot_real = weights * jnp.sum(
        amp_real[:, None] * map_real + amp_imag[:, None] * map_imag, axis=0
    )
    cot_imag = weights * jnp.sum(
        amp_real[:, None] * map_imag - amp_imag[:, None] * map_real, axis=0
    )
    return jnp.concatenate([cot_real, cot_imag], axis=0).astype(jnp.bfloat16)


def cotangent_rows(fields, farmap, weights):
    amp_real, amp_imag = amplitude_parts(fields, farmap)
    return cotangent_from(amp_real, amp_imag, farmap, weights)


def stacked_rows(adjoint, vectors):
    order_count = adjoint.shape[0] // 2
    widened = adjoint.astype(jnp.float32)
    scaled = [(vectors[axis_id][None, :] * widened).astype(jnp.bfloat16) for axis_id in range(3)]
    real_parts = [adjoint[:order_count]] + [item[:order_count] for item in scaled]
    imag_parts = [adjoint[order_count:]] + [item[order_count:] for item in scaled]
    return jnp.concatenate(real_parts + imag_parts, axis=0)


def gradients(output, coef_block):
    order_count = coef_block.shape[0] // 2
    real_out = output[: 4 * order_count]
    imag_out = output[4 * order_count :]
    coef_term = jnp.concatenate(
        [2.0 * real_out[:order_count], -2.0 * imag_out[:order_count]], axis=0
    )
    coef_real = coef_block[:order_count].astype(jnp.float32)
    coef_imag = coef_block[order_count:].astype(jnp.float32)
    place_terms = []
    for axis_id in range(3):
        lower_row = (axis_id + 1) * order_count
        upper_row = (axis_id + 2) * order_count
        place_terms.append(
            2.0
            * jnp.sum(
                coef_real * imag_out[lower_row:upper_row]
                + coef_imag * real_out[lower_row:upper_row],
                axis=0,
            )
        )
    return (coef_term, jnp.stack(place_terms))


def body(coefficients, positions, polar, azimuth, weights, farmap):
    own_count = coefficients.shape[2]
    own_rows = coefficients.reshape(2 * C, own_count)
    domain_rows = lax.all_gather(own_rows, "dir", axis=1, tiled=True)
    domain_places = lax.all_gather(positions, "dir", axis=1, tiled=True)
    vectors = unit_vectors(polar, azimuth)
    width_all = domain_rows.shape[1]
    width_block = 512
    blocks = width_all // width_block

    def forward_block(block_id, totals):
        offset = block_id * width_block
        coef_block = lax.dynamic_slice_in_dim(domain_rows, offset, width_block, 1)
        place_block = lax.dynamic_slice_in_dim(domain_places, offset, width_block, 1)
        cos_tile, sin_tile = phase_tile(place_block, vectors)
        return totals + field_terms(coef_block, cos_tile, sin_tile)

    partial_fields = lax.fori_loop(
        0, blocks, forward_block, jnp.zeros((2 * C, polar.shape[0]), jnp.float32)
    )
    fields = lax.psum(partial_fields, "dom")
    adjoint = cotangent_rows(fields, farmap, weights)
    stacked = stacked_rows(adjoint, vectors)

    def backward_block(block_id):
        offset = block_id * width_block
        coef_block = lax.dynamic_slice_in_dim(domain_rows, offset, width_block, 1)
        place_block = lax.dynamic_slice_in_dim(domain_places, offset, width_block, 1)
        cos_tile, sin_tile = phase_tile(place_block, vectors)
        return gradients(adjoint_terms(stacked, cos_tile, sin_tile), coef_block)

    coef_parts, place_parts = lax.map(backward_block, jnp.arange(blocks, dtype=jnp.int32))
    coef_part = jnp.moveaxis(coef_parts, 0, 1).reshape(2 * C, width_all)
    place_part = jnp.moveaxis(place_parts, 0, 1).reshape(3, width_all)
    coef_grad, place_grad = (
        lax.psum_scatter(coef_part, "dir", scatter_dimension=1, tiled=True),
        lax.psum_scatter(place_part, "dir", scatter_dimension=1, tiled=True),
    )
    return (coef_grad.reshape(2, C, own_count), place_grad)


def solution(mesh):
    placed = (
        P(None, None, ("dom", "dir")),
        P(None, ("dom", "dir")),
        P("dir"),
        P("dir"),
        P("dir"),
        P(None, None, None, "dir"),
    )
    return jax.shard_map(
        body,
        mesh=mesh,
        in_specs=placed,
        out_specs=(P(None, None, ("dom", "dir")), P(None, ("dom", "dir"))),
        check_vma=False,
    )
```

profile of v0, /device:TPU:8, one launch (start us, length us, event | category | flops | bytes accessed | tf_op | source)
XLA Modules:
  0.0 478.9 jit_solution(2724014570653692775)
XLA Ops:
  7.2 0.7 fusion.36
  7.9 0.7 sine_multiply_fusion
  8.7 0.8 copy.18
  9.5 50.1 %all_gather.7 = bf16[140,2048]{1,0:T(8,128)(2,1)S(1)} all-gather(bf16[140,128]{1,0:T(8,128)(2,1)S(1)} %reshape.65), channel_id=1, replica_groups=mesh['dom'=16,'dir'=16] {'dir'}, dimensions={1}, use_global_device_ids=true | all-gather | bytes 609280 | tf_op jit(solution)/shard_map/all_gather | solution.py:111
  59.6 38.4 %all_gather.6 = f32[3,2048]{1,0:T(4,128)S(1)} all-gather(f32[3,128]{1,0:T(4,128)} %param.11), channel_id=1, replica_groups=mesh['dom'=16,'dir'=16] {'dir'}, dimensions={1}, use_global_device_ids=true | all-gather | bytes 26112 | tf_op jit(solution)/shard_map/all_gather | solution.py:112
  98.0 24.7 %while.29 = (s32[]{:T(128)}, f32[140,640]{1,0:T(8,128)S(1)}, bf16[140,2048]{1,0:T(8,128)(2,1)S(1)}, f32[3,2048]{1,0:T(4,128)S(1)}, f32[1,640]{1,0:T(1,128)S(1)},...) while((s32[]{:T(128)}, f32[140,640]{1,0:T(8,128)S(1)}, ...), condition=%wide.region_1.0_spmd.clone, body=%wide.region_0.0_spmd.clone.sunk | while | flops 189849616 | bytes 3953417 | solution.py:125
  98.2 5.4 %cosine_convert_fusion.5 = (bf16[512,640]{1,0:T(8,128)(2,1)S(1)}, bf16[512,640]{1,0:T(8,128)(2,1)S(1)}) fusion(f32[640]{0:T(1024)S(1)} %reduce.15, f32[512]{0:T(512)S(1)} %bitcast.83, f32[640]{0:T(1024)S(1)} %reduce.16, f32[512]{0:T(512)S(1)} %bitcast.82, f32[640]{0:T(1024)S(1)} %reduce.17, f32[512]{0:T(512)S(1)} %bitcast.81), kind=kLoop, calls=%fused_computation.35.clone.1 | loop fusion | flops 2293760 | bytes 1324544 | tf_op jit(solution)/shard_map/while/body/eval_jaxpr/convert_element_type | solution.py:20
  103.7 0.4 fusion.55
  104.3 5.4 %cosine_convert_fusion.5 = (bf16[512,640]{1,0:T(8,128)(2,1)S(1)}, bf16[512,640]{1,0:T(8,128)(2,1)S(1)}) fusion(f32[640]{0:T(1024)S(1)} %reduce.15, f32[512]{0:T(512)S(1)} %bitcast.83, f32[640]{0:T(1024)S(1)} %reduce.16, f32[512]{0:T(512)S(1)} %bitcast.82, f32[640]{0:T(1024)S(1)} %reduce.17, f32[512]{0:T(512)S(1)} %bitcast.81), kind=kLoop, calls=%fused_computation.35.clone.1 | loop fusion | flops 2293760 | bytes 1324544 | tf_op jit(solution)/shard_map/while/body/eval_jaxpr/convert_element_type | solution.py:20
  109.9 0.4 fusion.55
  110.5 5.4 %cosine_convert_fusion.5 = (bf16[512,640]{1,0:T(8,128)(2,1)S(1)}, bf16[512,640]{1,0:T(8,128)(2,1)S(1)}) fusion(f32[640]{0:T(1024)S(1)} %reduce.15, f32[512]{0:T(512)S(1)} %bitcast.83, f32[640]{0:T(1024)S(1)} %reduce.16, f32[512]{0:T(512)S(1)} %bitcast.82, f32[640]{0:T(1024)S(1)} %reduce.17, f32[512]{0:T(512)S(1)} %bitcast.81), kind=kLoop, calls=%fused_computation.35.clone.1 | loop fusion | flops 2293760 | bytes 1324544 | tf_op jit(solution)/shard_map/while/body/eval_jaxpr/convert_element_type | solution.py:20
  116.1 0.4 fusion.55
  116.7 5.4 %cosine_convert_fusion.5 = (bf16[512,640]{1,0:T(8,128)(2,1)S(1)}, bf16[512,640]{1,0:T(8,128)(2,1)S(1)}) fusion(f32[640]{0:T(1024)S(1)} %reduce.15, f32[512]{0:T(512)S(1)} %bitcast.83, f32[640]{0:T(1024)S(1)} %reduce.16, f32[512]{0:T(512)S(1)} %bitcast.82, f32[640]{0:T(1024)S(1)} %reduce.17, f32[512]{0:T(512)S(1)} %bitcast.81), kind=kLoop, calls=%fused_computation.35.clone.1 | loop fusion | flops 2293760 | bytes 1324544 | tf_op jit(solution)/shard_map/while/body/eval_jaxpr/convert_element_type | solution.py:20
  122.2 0.4 fusion.55
  122.7 0.7 copy-done.1
  123.4 0.2 reduce-scatter.7.cloned.1.call-start
  123.7 0.6 fusion.31
  124.3 113.6 %all-reduce.2.cloned.1.call-done = f32[140,640]{1,0:T(8,128)} async-done(((f32[140,640]{1,0:T(8,128)}), f32[140,640]{1,0:T(8,128)}) %all-reduce.2.cloned.1.call-update) | async-done | bytes 358416 | tf_op jit(solution)/shard_map/psum | solution.py:128
  237.9 1.0 fusion.32
  239.5 14.7 %maximum_maximum_fusion = bf16[560,1280]{1,0:T(8,128)(2,1)S(1)} fusion(bf16[280,640]{1,0:T(8,128)(2,1)S(1)} %maximum_negate_fusion, bf16[70,640]{1,0:T(8,128)(2,1)S(1)} %get-tuple-element.343, bf16[70,640]{1,0:T(8,128)(2,1)S(1)} %get-tuple-element.355, bf16[70,640]{1,0:T(8,128)(2,1)S(1)} %get-tuple-element.339, bf16[70,640]{1,0:T(8,128)(2,1)S(1)} %get-tuple-element.351, ...), kind=kLoop, calls=%fused_computation.48 | loop fusion | flops 18636800 | bytes 2508800 | tf_op jit(solution)/shard_map/while/body/eval_jaxpr/concatenate | solution.py:40
  254.2 35.1 %while.28 = (s32[]{:T(128)}, f32[4,140,512]{2,1,0:T(8,128)}, f32[4,3,512]{2,1,0:T(4,128)S(1)}, s32[4]{0:T(128)S(1)}, f32[3,2048]{1,0:T(4,128)S(1)}, /*index=5*/f...) while((s32[]{:T(128)}, f32[4,140,512]{2,1,0:T(8,128)}, ...), condition=%wide.region_11.12_spmd, body=%wide.region_7.11_spmd.sunk | while | flops 739566592 | bytes 7435559 | solution.py:139
  254.2 0.6 dynamic_slice.33
  255.6 5.4 %cosine_convert_fusion.4 = (bf16[512,640]{1,0:T(8,128)(2,1)S(1)}, bf16[512,640]{1,0:T(8,128)(2,1)S(1)}) fusion(f32[640]{0:T(1024)S(1)} %reduce.12, f32[512]{0:T(512)S(1)} %bitcast.86, f32[640]{0:T(1024)S(1)} %reduce.13, f32[512]{0:T(512)S(1)} %bitcast.85, f32[640]{0:T(1024)S(1)} %reduce.14, f32[512]{0:T(512)S(1)} %bitcast.84), kind=kLoop, calls=%fused_computation.5.clone.1 | loop fusion | flops 2293760 | bytes 1324544 | tf_op jit(solution)/shard_map/while/body/eval_jaxpr/convert_element_type | solution.py:20
  261.1 0.9 convolution_bitcast_fusion.2
  262.0 0.2 fusion.49
  262.3 0.7 fusion.50
  263.0 0.6 dynamic_slice.33
  264.4 5.4 %cosine_convert_fusion.4 = (bf16[512,640]{1,0:T(8,128)(2,1)S(1)}, bf16[512,640]{1,0:T(8,128)(2,1)S(1)}) fusion(f32[640]{0:T(1024)S(1)} %reduce.12, f32[512]{0:T(512)S(1)} %bitcast.86, f32[640]{0:T(1024)S(1)} %reduce.13, f32[512]{0:T(512)S(1)} %bitcast.85, f32[640]{0:T(1024)S(1)} %reduce.14, f32[512]{0:T(512)S(1)} %bitcast.84), kind=kLoop, calls=%fused_computation.5.clone.1 | loop fusion | flops 2293760 | bytes 1324544 | tf_op jit(solution)/shard_map/while/body/eval_jaxpr/convert_element_type | solution.py:20
  269.9 0.9 convolution_bitcast_fusion.2
  270.8 0.2 fusion.49
  271.1 0.7 fusion.50
  271.8 0.6 dynamic_slice.33
  273.2 5.4 %cosine_convert_fusion.4 = (bf16[512,640]{1,0:T(8,128)(2,1)S(1)}, bf16[512,640]{1,0:T(8,128)(2,1)S(1)}) fusion(f32[640]{0:T(1024)S(1)} %reduce.12, f32[512]{0:T(512)S(1)} %bitcast.86, f32[640]{0:T(1024)S(1)} %reduce.13, f32[512]{0:T(512)S(1)} %bitcast.85, f32[640]{0:T(1024)S(1)} %reduce.14, f32[512]{0:T(512)S(1)} %bitcast.84), kind=kLoop, calls=%fused_computation.5.clone.1 | loop fusion | flops 2293760 | bytes 1324544 | tf_op jit(solution)/shard_map/while/body/eval_jaxpr/convert_element_type | solution.py:20
  278.6 0.9 convolution_bitcast_fusion.2
  279.6 0.2 fusion.49
  279.9 0.7 fusion.50
  280.6 0.6 dynamic_slice.33
  282.0 5.4 %cosine_convert_fusion.4 = (bf16[512,640]{1,0:T(8,128)(2,1)S(1)}, bf16[512,640]{1,0:T(8,128)(2,1)S(1)}) fusion(f32[640]{0:T(1024)S(1)} %reduce.12, f32[512]{0:T(512)S(1)} %bitcast.86, f32[640]{0:T(1024)S(1)} %reduce.13, f32[512]{0:T(512)S(1)} %bitcast.85, f32[640]{0:T(1024)S(1)} %reduce.14, f32[512]{0:T(512)S(1)} %bitcast.84), kind=kLoop, calls=%fused_computation.5.clone.1 | loop fusion | flops 2293760 | bytes 1324544 | tf_op jit(solution)/shard_map/while/body/eval_jaxpr/convert_element_type | solution.py:20
  287.4 0.9 convolution_bitcast_fusion.2
  288.6 0.7 fusion.50
  289.4 1.4 copy.23
  290.8 2.0 copy.20
  293.1 1.4 copy.27
  294.5 87.7 %reduce-scatter.7.cloned.1.call-done = f32[128,3]{1,0:T(8,128)} async-done(((f32[2048,3]{1,0:T(8,128)}), f32[128,3]{1,0:T(8,128)}) %reduce-scatter.7.cloned.1.call-update) | async-done | bytes 1552
  382.2 1.5 copy.24
  383.7 87.1 %reduce-scatter.5.cloned.1.call-done = f32[140,128]{1,0:T(8,128)} async-done(((f32[140,2048]{1,0:T(8,128)}), f32[140,128]{1,0:T(8,128)}) %reduce-scatter.5.cloned.1.call-update) | async-done | bytes 71696 | tf_op jit(solution)/shard_map/reduce_scatter | solution.py:143
  470.8 0.9 reshape.67
  471.7 0.7 copy.22
  (75 shorter events, 2.7 us)
Async XLA Ops:
  7.2 230.7 %all-reduce.2.cloned.1.call-start = ((), (), s32[]{:S(2)}) async-start(), calls=%async_computation.2 | async-start | bytes 737280 | tf_op jit(solution)/shard_map/psum | solution.py:128
  98.0 25.7 %copy-start = (f32[2,2,70,640]{3,1,2,0:T(2,128)S(1)}, f32[2,2,70,640]{3,1,2,0:T(2,128)}, u32[]{:S(2)}) copy-start(f32[2,2,70,640]{3,1,2,0:T(2,128)} %param.15) | copy-start | bytes 2150404
  122.7 0.7 copy-start.1
  123.4 258.8 %reduce-scatter.7.cloned.1.call-start = ((), (), s32[]{:S(2)}) async-start(), calls=%async_computation.4 | async-start | bytes 1114112
  124.3 114.9 %copy-start.2 = (f32[640]{0:T(1024)S(1)}, f32[640]{0:T(1024)}, u32[]{:S(2)}) copy-start(f32[640]{0:T(1024)} %param.14) | copy-start | bytes 7684
  290.8 180.0 %reduce-scatter.5.cloned.1.call-start = ((), (), s32[]{:S(2)}) async-start(), calls=%async_computation.3 | async-start | bytes 1253376 | tf_op jit(solution)/shard_map/reduce_scatter | solution.py:143
Sparse Core Ops, SparseCore 0:
  123.6 114.2 all-reduce.1
  290.9 91.2 reduce-scatter.6
  385.7 85.0 reduce-scatter.4
where the time goes:
time: 479 us
  waiting for transfers between devices  288 us (60%)
  blocking collectives  88.5 us (18%)
  other arithmetic  64.2 us (13%)
  local copies, waits for them, and re-layouts  15 us (3%)
  between operations  13.9 us (3%)
  matrix products  5.45 us (1%)
    psum x1, waiting for transfers between devices, body(): fields = lax.psum(partial_fields, 'dom')  114 us
    unnamed x4, waiting for transfers between devices  87.7 us
    reduce_scatter x1, waiting for transfers between devices, body(): lax.psum_scatter(coef_part, 'dir', scatter_dimension=1, tiled=True)  87.1 us
    all_gather x1, blocking collectives, body(): domain_rows = lax.all_gather(own_rows, 'dir', axis=1, tiled=True)  50.1 us
    convert_element_type x8, other arithmetic, phase_tile(): jnp.cos(angles).astype(jnp.bfloat16)  43.5 us
    all_gather x1, blocking collectives, body(): domain_places = lax.all_gather(positions, 'dir', axis=1, tiled=True)  38.4 us
    concatenate x1, other arithmetic, adjoint_terms(): left_side = jnp.concatenate([top_rows, low_rows], axis=0)  14.7 us
  transfers between devices with their start and end apart: 3, of which 3 were waited for; matrix products, arithmetic and copies ran while one was open for 1% of the time, Pallas kernels for 0%

commit v1 on v0

--- a/solution.py
+++ b/solution.py
@@ -108,7 +108,9 @@
 def body(coefficients, positions, polar, azimuth, weights, farmap):
     own_count = coefficients.shape[2]
     own_rows = coefficients.reshape(2 * C, own_count)
-    domain_rows = lax.all_gather(own_rows, "dir", axis=1, tiled=True)
+    domain_rows = jnp.concatenate(
+        lax.all_to_all(jnp.stack([own_rows] * lax.axis_size("dir")), "dir", 0, 0), axis=1
+    )
     domain_places = lax.all_gather(positions, "dir", axis=1, tiled=True)
     vectors = unit_vectors(polar, azimuth)
     width_all = domain_rows.shape[1]

time: 479 us -> 450 us (0.939)
  blocking collectives: 88.5 us -> 50.6 us
  starting transfers between devices: 0.3 us -> 11.3 us
    all_gather x1 -> x0, blocking collectives: 50.1 us -> none  [body(): domain_rows = lax.all_gather(own_rows, 'dir', axis=1, tiled=True)]
    all_gather x1, blocking collectives: 38.4 us -> 50.6 us  [body(): domain_places = lax.all_gather(positions, 'dir', axis=1, tiled=True)]
    all_to_all x0 -> x1, starting transfers between devices: none -> 11 us  [body(): lax.all_to_all(jnp.stack([own_rows] * lax.axis_size('dir')), 'dir', 0, 0)]
  transfers between devices with their start and end apart: 3 -> 4, of which waited for: 3 -> 3; matrix products, arithmetic and copies ran while one was open for 1% -> 1% of each run, Pallas kernels for 0% -> 0%
where the time goes in v1:
time: 450 us
  waiting for transfers between devices  286 us (64%)
  other arithmetic  63.5 us (14%)
  blocking collectives  50.6 us (11%)
  local copies, waits for them, and re-layouts  15.7 us (3%)
  between operations  14 us (3%)
  starting transfers between devices  11.3 us (3%)
  matrix products  5.45 us (1%)
    psum x1, waiting for transfers between devices, body(): fields = lax.psum(partial_fields, 'dom')  111 us
    unnamed x4, waiting for transfers between devices  87.9 us
    reduce_scatter x1, waiting for transfers between devices, body(): lax.psum_scatter(coef_part, 'dir', scatter_dimension=1, tiled=True)  87.1 us
    all_gather x1, blocking collectives, body(): domain_places = lax.all_gather(positions, 'dir', axis=1, tiled=True)  50.6 us
    convert_element_type x8, other arithmetic, phase_tile(): jnp.cos(angles).astype(jnp.bfloat16)  43.6 us
    concatenate x1, other arithmetic, adjoint_terms(): left_side = jnp.concatenate([top_rows, low_rows], axis=0)  14.7 us
    all_to_all x1, starting transfers between devices, body(): lax.all_to_all(jnp.stack([own_rows] * lax.axis_size('dir')), 'dir', 0, 0)  11 us
  transfers between devices with their start and end apart: 4, of which 3 were waited for; matrix products, arithmetic and copies ran while one was open for 1% of the time, Pallas kernels for 0%

profile of v1, /device:TPU:8, one launch (start us, length us, event | category | flops | bytes accessed | tf_op | source)
XLA Modules:
  0.0 449.8 jit_solution(11085063543772548002)
XLA Ops:
  7.2 0.8 copy.23
  8.0 0.9 stack.23
  8.9 11.0 %all-to-all-start = ((bf16[16,140,128]{2,1,0:T(8,128)(2,1)}), bf16[16,140,128]{2,1,0:T(8,128)(2,1)S(1)}, u32[]{:S(2)}, u32[]{:S(2)}) async-start(bf16[16,140,128]{2,1,0:T(8,128)(2,1)} %stack.23), calls=%async_computation | async-start | bytes 1179648 | tf_op jit(solution)/shard_map/all_to_all | solution.py:112
  20.1 50.6 %all_gather.3 = f32[3,2048]{1,0:T(4,128)S(1)} all-gather(f32[3,128]{1,0:T(4,128)S(1)} %copy-done.5), channel_id=1, replica_groups=mesh['dom'=16,'dir'=16] {'dir'}, dimensions={1}, use_global_device_ids=true | all-gather | bytes 26112 | tf_op jit(solution)/shard_map/all_gather | solution.py:114
  71.2 24.7 %while.29 = (s32[]{:T(128)}, f32[140,640]{1,0:T(8,128)S(1)}, bf16[140,2048]{1,0:T(8,128)(2,1)S(1)}, f32[3,2048]{1,0:T(4,128)S(1)}, f32[1,640]{1,0:T(1,128)S(1)},...) while((s32[]{:T(128)}, f32[140,640]{1,0:T(8,128)S(1)}, ...), condition=%wide.region_1.0_spmd.clone, body=%wide.region_0.0_spmd.clone.sunk | while | flops 189849616 | bytes 3953417 | solution.py:127
  71.3 5.4 %cosine_convert_fusion.5 = (bf16[512,640]{1,0:T(8,128)(2,1)S(1)}, bf16[512,640]{1,0:T(8,128)(2,1)S(1)}) fusion(f32[640]{0:T(1024)S(1)} %reduce.15, f32[512]{0:T(512)S(1)} %bitcast.90, f32[640]{0:T(1024)S(1)} %reduce.16, f32[512]{0:T(512)S(1)} %bitcast.89, f32[640]{0:T(1024)S(1)} %reduce.17, f32[512]{0:T(512)S(1)} %bitcast.88), kind=kLoop, calls=%fused_computation.35.clone.1 | loop fusion | flops 2293760 | bytes 1324544 | tf_op jit(solution)/shard_map/while/body/eval_jaxpr/convert_element_type | solution.py:20
  76.9 0.4 fusion.55
  77.5 5.4 %cosine_convert_fusion.5 = (bf16[512,640]{1,0:T(8,128)(2,1)S(1)}, bf16[512,640]{1,0:T(8,128)(2,1)S(1)}) fusion(f32[640]{0:T(1024)S(1)} %reduce.15, f32[512]{0:T(512)S(1)} %bitcast.90, f32[640]{0:T(1024)S(1)} %reduce.16, f32[512]{0:T(512)S(1)} %bitcast.89, f32[640]{0:T(1024)S(1)} %reduce.17, f32[512]{0:T(512)S(1)} %bitcast.88), kind=kLoop, calls=%fused_computation.35.clone.1 | loop fusion | flops 2293760 | bytes 1324544 | tf_op jit(solution)/shard_map/while/body/eval_jaxpr/convert_element_type | solution.py:20
  83.1 0.4 fusion.55
  83.7 5.4 %cosine_convert_fusion.5 = (bf16[512,640]{1,0:T(8,128)(2,1)S(1)}, bf16[512,640]{1,0:T(8,128)(2,1)S(1)}) fusion(f32[640]{0:T(1024)S(1)} %reduce.15, f32[512]{0:T(512)S(1)} %bitcast.90, f32[640]{0:T(1024)S(1)} %reduce.16, f32[512]{0:T(512)S(1)} %bitcast.89, f32[640]{0:T(1024)S(1)} %reduce.17, f32[512]{0:T(512)S(1)} %bitcast.88), kind=kLoop, calls=%fused_computation.35.clone.1 | loop fusion | flops 2293760 | bytes 1324544 | tf_op jit(solution)/shard_map/while/body/eval_jaxpr/convert_element_type | solution.py:20
  89.2 0.4 fusion.55
  89.8 5.4 %cosine_convert_fusion.5 = (bf16[512,640]{1,0:T(8,128)(2,1)S(1)}, bf16[512,640]{1,0:T(8,128)(2,1)S(1)}) fusion(f32[640]{0:T(1024)S(1)} %reduce.15, f32[512]{0:T(512)S(1)} %bitcast.90, f32[640]{0:T(1024)S(1)} %reduce.16, f32[512]{0:T(512)S(1)} %bitcast.89, f32[640]{0:T(1024)S(1)} %reduce.17, f32[512]{0:T(512)S(1)} %bitcast.88), kind=kLoop, calls=%fused_computation.35.clone.1 | loop fusion | flops 2293760 | bytes 1324544 | tf_op jit(solution)/shard_map/while/body/eval_jaxpr/convert_element_type | solution.py:20
  95.4 0.4 fusion.55
  95.9 0.7 copy-done.1
  96.6 0.2 reduce-scatter.7.cloned.1.call-start
  96.9 0.6 fusion.31
  97.5 111.1 %all-reduce.2.cloned.1.call-done = f32[140,640]{1,0:T(8,128)} async-done(((f32[140,640]{1,0:T(8,128)}), f32[140,640]{1,0:T(8,128)}) %all-reduce.2.cloned.1.call-update) | async-done | bytes 358416 | tf_op jit(solution)/shard_map/psum | solution.py:130
  208.6 1.0 fusion.32
  210.2 14.7 %maximum_maximum_fusion = bf16[560,1280]{1,0:T(8,128)(2,1)S(1)} fusion(bf16[280,640]{1,0:T(8,128)(2,1)S(1)} %maximum_negate_fusion, bf16[70,640]{1,0:T(8,128)(2,1)S(1)} %get-tuple-element.345, bf16[70,640]{1,0:T(8,128)(2,1)S(1)} %get-tuple-element.357, bf16[70,640]{1,0:T(8,128)(2,1)S(1)} %get-tuple-element.341, bf16[70,640]{1,0:T(8,128)(2,1)S(1)} %get-tuple-element.353, ...), kind=kLoop, calls=%fused_computation.48 | loop fusion | flops 18636800 | bytes 2508800 | tf_op jit(solution)/shard_map/while/body/eval_jaxpr/concatenate | solution.py:40
  224.9 35.2 %while.28 = (s32[]{:T(128)}, f32[4,140,512]{2,1,0:T(8,128)}, f32[4,3,512]{2,1,0:T(4,128)S(1)}, s32[4]{0:T(128)S(1)}, f32[3,2048]{1,0:T(4,128)S(1)}, /*index=5*/f...) while((s32[]{:T(128)}, f32[4,140,512]{2,1,0:T(8,128)}, ...), condition=%wide.region_11.12_spmd, body=%wide.region_7.11_spmd.sunk | while | flops 739566592 | bytes 7435559 | solution.py:141
  225.0 0.6 dynamic_slice.33
  226.3 5.5 %cosine_convert_fusion.4 = (bf16[512,640]{1,0:T(8,128)(2,1)S(1)}, bf16[512,640]{1,0:T(8,128)(2,1)S(1)}) fusion(f32[640]{0:T(1024)S(1)} %reduce.12, f32[512]{0:T(512)S(1)} %bitcast.93, f32[640]{0:T(1024)S(1)} %reduce.13, f32[512]{0:T(512)S(1)} %bitcast.92, f32[640]{0:T(1024)S(1)} %reduce.14, f32[512]{0:T(512)S(1)} %bitcast.91), kind=kLoop, calls=%fused_computation.5.clone.1 | loop fusion | flops 2293760 | bytes 1324544 | tf_op jit(solution)/shard_map/while/body/eval_jaxpr/convert_element_type | solution.py:20
  231.8 0.9 convolution_bitcast_fusion.2
  232.7 0.2 fusion.49
  233.0 0.7 fusion.50
  233.8 0.6 dynamic_slice.33
  235.1 5.5 %cosine_convert_fusion.4 = (bf16[512,640]{1,0:T(8,128)(2,1)S(1)}, bf16[512,640]{1,0:T(8,128)(2,1)S(1)}) fusion(f32[640]{0:T(1024)S(1)} %reduce.12, f32[512]{0:T(512)S(1)} %bitcast.93, f32[640]{0:T(1024)S(1)} %reduce.13, f32[512]{0:T(512)S(1)} %bitcast.92, f32[640]{0:T(1024)S(1)} %reduce.14, f32[512]{0:T(512)S(1)} %bitcast.91), kind=kLoop, calls=%fused_computation.5.clone.1 | loop fusion | flops 2293760 | bytes 1324544 | tf_op jit(solution)/shard_map/while/body/eval_jaxpr/convert_element_type | solution.py:20
  240.6 0.9 convolution_bitcast_fusion.2
  241.5 0.2 fusion.49
  241.8 0.7 fusion.50
  242.5 0.6 dynamic_slice.33
  243.9 5.5 %cosine_convert_fusion.4 = (bf16[512,640]{1,0:T(8,128)(2,1)S(1)}, bf16[512,640]{1,0:T(8,128)(2,1)S(1)}) fusion(f32[640]{0:T(1024)S(1)} %reduce.12, f32[512]{0:T(512)S(1)} %bitcast.93, f32[640]{0:T(1024)S(1)} %reduce.13, f32[512]{0:T(512)S(1)} %bitcast.92, f32[640]{0:T(1024)S(1)} %reduce.14, f32[512]{0:T(512)S(1)} %bitcast.91), kind=kLoop, calls=%fused_computation.5.clone.1 | loop fusion | flops 2293760 | bytes 1324544 | tf_op jit(solution)/shard_map/while/body/eval_jaxpr/convert_element_type | solution.py:20
  249.4 0.9 convolution_bitcast_fusion.2
  250.3 0.2 fusion.49
  250.6 0.7 fusion.50
  251.3 0.6 dynamic_slice.33
  252.7 5.5 %cosine_convert_fusion.4 = (bf16[512,640]{1,0:T(8,128)(2,1)S(1)}, bf16[512,640]{1,0:T(8,128)(2,1)S(1)}) fusion(f32[640]{0:T(1024)S(1)} %reduce.12, f32[512]{0:T(512)S(1)} %bitcast.93, f32[640]{0:T(1024)S(1)} %reduce.13, f32[512]{0:T(512)S(1)} %bitcast.92, f32[640]{0:T(1024)S(1)} %reduce.14, f32[512]{0:T(512)S(1)} %bitcast.91), kind=kLoop, calls=%fused_computation.5.clone.1 | loop fusion | flops 2293760 | bytes 1324544 | tf_op jit(solution)/shard_map/while/body/eval_jaxpr/convert_element_type | solution.py:20
  258.2 0.9 convolution_bitcast_fusion.2
  259.1 0.2 fusion.49
  259.4 0.7 fusion.50
  260.1 1.4 copy.29
  261.6 2.0 copy.26
  263.8 1.4 copy.34
  265.3 87.9 %reduce-scatter.7.cloned.1.call-done = f32[128,3]{1,0:T(8,128)} async-done(((f32[2048,3]{1,0:T(8,128)}), f32[128,3]{1,0:T(8,128)}) %reduce-scatter.7.cloned.1.call-update) | async-done | bytes 1552
  353.1 1.5 copy.30
  354.6 87.1 %reduce-scatter.5.cloned.1.call-done = f32[140,128]{1,0:T(8,128)} async-done(((f32[140,2048]{1,0:T(8,128)}), f32[140,128]{1,0:T(8,128)}) %reduce-scatter.5.cloned.1.call-update) | async-done | bytes 71696 | tf_op jit(solution)/shard_map/reduce_scatter | solution.py:145
  441.7 0.9 reshape.73
  442.6 0.7 copy.28
  (86 shorter events, 3.1 us)
Async XLA Ops:
  7.2 12.8 %copy-start.3 = (f32[640]{0:T(1024)S(1)}, f32[640]{0:T(1024)}, u32[]{:S(2)}) copy-start(f32[640]{0:T(1024)} %param.12) | copy-start | bytes 7684
  7.2 12.9 %copy-start.4 = (f32[640]{0:T(1024)S(1)}, f32[640]{0:T(1024)}, u32[]{:S(2)}) copy-start(f32[640]{0:T(1024)} %param.13) | copy-start | bytes 7684
  7.2 12.9 %copy-start.5 = (f32[3,128]{1,0:T(4,128)S(1)}, f32[3,128]{1,0:T(4,128)}, u32[]{:S(2)}) copy-start(f32[3,128]{1,0:T(4,128)} %param.11) | copy-start | bytes 4612
  8.9 61.8 %all-to-all-start = ((bf16[16,140,128]{2,1,0:T(8,128)(2,1)}), bf16[16,140,128]{2,1,0:T(8,128)(2,1)S(1)}, u32[]{:S(2)}, u32[]{:S(2)}) async-start(bf16[16,140,128]{2,1,0:T(8,128)(2,1)} %stack.23), calls=%async_computation | async-start | bytes 1179648 | tf_op jit(solution)/shard_map/all_to_all | solution.py:112
  19.9 188.6 %all-reduce.2.cloned.1.call-start = ((), (), s32[]{:S(2)}) async-start(), calls=%async_computation.3 | async-start | bytes 737280 | tf_op jit(solution)/shard_map/psum | solution.py:130
  71.2 25.7 %copy-start = (f32[2,2,70,640]{3,1,2,0:T(2,128)S(1)}, f32[2,2,70,640]{3,1,2,0:T(2,128)}, u32[]{:S(2)}) copy-start(f32[2,2,70,640]{3,1,2,0:T(2,128)} %param.15) | copy-start | bytes 2150404
  95.9 0.7 copy-start.1
  96.6 256.5 %reduce-scatter.7.cloned.1.call-start = ((), (), s32[]{:S(2)}) async-start(), calls=%async_computation.5 | async-start | bytes 1114112
  97.4 112.4 %copy-start.2 = (f32[640]{0:T(1024)S(1)}, f32[640]{0:T(1024)}, u32[]{:S(2)}) copy-start(f32[640]{0:T(1024)} %param.14) | copy-start | bytes 7684
  261.6 180.2 %reduce-scatter.5.cloned.1.call-start = ((), (), s32[]{:S(2)}) async-start(), calls=%async_computation.4 | async-start | bytes 1253376 | tf_op jit(solution)/shard_map/reduce_scatter | solution.py:145
Sparse Core Ops, SparseCore 0:
  96.7 111.7 all-reduce.1
  261.7 91.3 reduce-scatter.6
  356.6 85.0 reduce-scatter.4
